TPU v7x, 256 devices: a whole 4x4x8 slice. The times are simulated.
256 devices in a mesh: lon: 32 (over z, y_lo, core), lat: 8 (over x, y_hi).
Axes of the slice: x: 4, y: 4 (y_hi: 2, y_lo: 2; y = y_hi * 2 + y_lo), z: 8, core: 2. Of those that a mesh axis runs over, the one named last changes fastest.
Arguments:
- embeddings: bfloat16 [512, 2048, 128], P('lat', 'lon'), may hold values from -400 to 400
- query_owner: int32 [2, 64], replicated, may hold values from 0 to 255
- query_row: int32 [2, 64], replicated, may hold values from 0 to 59
- query_col: int32 [2, 64], replicated, may hold values from 0 to 59
Outputs:
- scores: float32 [512, 2048, 128], P('lat', 'lon')
Inputs may be any that keep to these rules, and one draw needn't show every extreme that they name: `query_row`: the exemplar lies inside its owner's tile. `query_col`: the exemplar lies inside its owner's tile.
All inputs are finite; a program needn't handle non-finite values.
Results may differ from a plain program's by a relative error of at most 0.0029.
Values may be sent and summed in bfloat16 or wider, within the bound.
A program may use at most 128 MiB of HBM per device.

v0:
```python
import jax
import jax.numpy as jnp
from jax import lax
from jax.sharding import PartitionSpec as P


def extended_2(x, sides, width):
    for axis, dim in sides:
        count, length = (lax.axis_size(axis), x.shape[dim])
        up = [(i, (i + 1) % count) for i in range(count)]
        down = [(j, i) for i, j in up]
        last = lax.slice_in_dim(x, length - width, length, axis=dim)
        first = lax.slice_in_dim(x, 0, width, axis=dim)
        before = lax.ppermute(last, axis, up)
        after = lax.ppermute(first, axis, down)
        x = jnp.concatenate([before, x, after], axis=dim)
    return x


def body(embeddings, query_owner, query_row, query_col):
    rows, cols, chans = embeddings.shape
    band = lax.axis_index("lat")
    strip = lax.axis_index("lon")
    here = band * lax.axis_size("lon") + strip
    owner = query_owner.reshape(-1)
    row_first = query_row.reshape(-1)
    col_first = query_col.reshape(-1)

    def take(row_one, col_one):
        zero = jnp.zeros((), jnp.int32)
        return lax.dynamic_slice(embeddings, (row_one, col_one, zero), (5, 5, chans))

    patches = jax.vmap(take, out_axes=3)(row_first, col_first).astype(jnp.float32)
    count = patches.shape[3]
    table = jnp.where((owner == here)[None, None, None, :], patches, 0.0)
    whole = lax.psum(table, ("lon", "lat"))
    mean_sq = jnp.mean(whole * whole, axis=(0, 1, 2))
    queries = (whole * lax.rsqrt(mean_sq + 1e-05)).astype(jnp.bfloat16)
    extended = extended_2(embeddings, (("lat", 0), ("lon", 1)), 2)
    row_index = jnp.arange(rows + 4, dtype=jnp.int32)[:, None, None]
    cut_top = (band == 0) & (row_index < 2)
    cut_bottom = (band == lax.axis_size("lat") - 1) & (row_index >= rows + 2)
    extended = jnp.where(cut_top | cut_bottom, jnp.zeros((), jnp.bfloat16), extended)
    total = jnp.zeros((rows * cols, count), jnp.float32)
    for shift_y in range(5):
        for shift_x in range(5):
            slab = extended[shift_y : shift_y + rows, shift_x : shift_x + cols, :].reshape(
                rows * cols, chans
            )
            total = total + jnp.dot(
                slab, queries[shift_y, shift_x], preferred_element_type=jnp.float32
            )
    squares = jnp.sum(jnp.square(extended.astype(jnp.float32)), axis=2)
    box_sum = jnp.zeros((rows, cols), jnp.float32)
    for shift_y in range(5):
        for shift_x in range(5):
            box_sum = box_sum + squares[shift_y : shift_y + rows, shift_x : shift_x + cols]
    energy = box_sum / (25 * chans)
    return total.reshape(rows, cols, count) * lax.rsqrt(25 * chans * (energy + 1e-05))[:, :, None]


def solution(mesh):
    placed = (P("lat", "lon", None), P(), P(), P())
    return jax.shard_map(
        body, mesh=mesh, in_specs=placed, out_specs=P("lat", "lon", None), check_vma=False
    )
```

profile of v0, /device:TPU:2, one launch (start us, length us, event | category | flops | bytes accessed | tf_op | source)
XLA Modules:
  0.0 670.3 jit_solution(10743078012196713790)
XLA Ops:
  7.3 3.2 collective-permute-start.1
  13.2 350.3 %while.1 = (s32[]{:T(128)}, bf16[64,64,128]{2,1,0:T(8,128)(2,1)}, s32[128,3]{0,1:T(4,128)S(1)}, bf16[128,5,5,128]{3,2,1,0:T(8,128)(2,1)S(1)}, s32[]{:T(128)}) while((s32[]{:T(128)}, bf16[64,64,128]{2,1,0:T(8,128)(2,1)}, s32[128,3]{0,1:T(4,128)S(1)}, bf16[128,5,5,128]{3,2,1,0:T(8,128)(2,1)S(1)}, s32[]{:T(128)}) %tuple.46), condition=%wide.while_cond, body=%wide.while_body.sunk | while | flops 2 | bytes 16765 | solution.py:31
  13.8 2.1 bitcast_dynamic-update-slice_fusion.2
  16.6 2.1 bitcast_dynamic-update-slice_fusion.2
  19.3 2.1 bitcast_dynamic-update-slice_fusion.2
  22.1 2.1 bitcast_dynamic-update-slice_fusion.2
  24.8 2.1 bitcast_dynamic-update-slice_fusion.2
  27.5 2.1 bitcast_dynamic-update-slice_fusion.2
  49.4 2.1 bitcast_dynamic-update-slice_fusion.2
  52.2 2.1 bitcast_dynamic-update-slice_fusion.2
  54.9 2.1 bitcast_dynamic-update-slice_fusion.2
  57.7 2.1 bitcast_dynamic-update-slice_fusion.2
  60.4 2.1 bitcast_dynamic-update-slice_fusion.2
  63.1 2.1 bitcast_dynamic-update-slice_fusion.2
  65.9 2.1 bitcast_dynamic-update-slice_fusion.2
  68.6 2.1 bitcast_dynamic-update-slice_fusion.2
  71.4 2.1 bitcast_dynamic-update-slice_fusion.2
  76.8 2.1 bitcast_dynamic-update-slice_fusion.2
  79.5 2.1 bitcast_dynamic-update-slice_fusion.2
  268.4 2.1 bitcast_dynamic-update-slice_fusion.2
  366.7 5.8 collective-permute-start.3
  375.8 3.4 fusion.7
  379.2 8.0 %fusion.6 = (bf16[64,64,128]{2,1,0:T(8,128)(2,1)S(1)}, bf16[64,64,128]{2,1,0:T(8,128)(2,1)S(1)}, bf16[64,64,128]{2,1,0:T(8,128)(2,1)S(1)}, bf16[64,64,128]{2,1,0...) fusion(bf16[68,68,128]{2,1,0:T(8,128)(2,1)S(1)} %get-tuple-elem, ...), kind=kLoop, calls=%fused_computation.96 | loop fusion | bytes 39845888 | tf_op jit(solution)/shard_map/slice | solution.py:47
  387.3 244.6 %all-reduce.2.cloned.1.call-done = f32[5,5,128,128]{3,2,1,0:T(8,128)} async-done(((f32[5,5,128,128]{3,2,1,0:T(8,128)}), f32[5,5,128,128]{3,2,1,0:T(8,128)}) %all-reduce.2.cloned.1.call-update) | async-done | bytes 1638416 | tf_op jit(solution)/shard_map/psum | solution.py:36
  (469 shorter events, 352.7 us)
Async XLA Ops:
  6.5 625.3 %all-reduce.2.cloned.1.call-start = ((), (), s32[]{:S(2)}) async-start(), calls=%async_computation | async-start | bytes 3276800 | tf_op jit(solution)/shard_map/psum | solution.py:36
  7.3 359.2 %collective-permute-start.1 = (bf16[2,64,128]{2,1,0:T(8,128)(2,1)S(1)}, bf16[2,64,128]{2,1,0:T(8,128)(2,1)S(1)}, u32[]{:S(2)}, u32[]{:S(2)}) collective-permute-start(bf16[2,64,128]{2,1,0:T(8,128)(2,1)S(1)} %get-tuple-element.52), channel_id=1, source_target_pairs={{1,0},{2,1},{3,2},{4,3},{5,4},{6,5},{7,6},{0,7},{9,8},{10,9},{11,1... | collective-permute-start | bytes 98312 | tf_op jit(solution)/shard_map/ppermute | solution.py:15
  10.5 355.8 %collective-permute-start = (bf16[2,64,128]{2,1,0:T(8,128)(2,1)S(1)}, bf16[2,64,128]{2,1,0:T(8,128)(2,1)S(1)}, u32[]{:S(2)}, u32[]{:S(2)}) collective-permute-start(bf16[2,64,128]{2,1,0:T(8,128)(2,1)S(1)} %get-tuple-element.53), channel_id=1, source_target_pairs={{0,1},{1,2},{2,3},{3,4},{4,5},{5,6},{6,7},{7,0},{8,9},{9,10},{10,1... | collective-permute-start | bytes 98312 | tf_op jit(solution)/shard_map/ppermute | solution.py:14
  364.9 1.5 copy-start.23
  366.6 7.4 %collective-permute-start.2 = (bf16[68,2,128]{2,1,0:T(2,128)(2,1)S(1)}, bf16[68,2,128]{2,1,0:T(2,128)(2,1)S(1)}, u32[]{:S(2)}, u32[]{:S(2)}) collective-permute-start(bf16[68,2,128]{2,1,0:T(2,128)(2,1)S(1)} %get-tuple-element.50), channel_id=1, source_target_pairs={{0,8},{8,16},{16,24},{24,32},{32,40},{40,48},{48,56},{56,64},{64,7... | collective-permute-start | bytes 104456 | tf_op jit(solution)/shard_map/ppermute | solution.py:14
  366.7 7.4 %collective-permute-start.3 = (bf16[68,2,128]{2,1,0:T(2,128)(2,1)S(1)}, bf16[68,2,128]{2,1,0:T(2,128)(2,1)S(1)}, u32[]{:S(2)}, u32[]{:S(2)}) collective-permute-start(bf16[68,2,128]{2,1,0:T(2,128)(2,1)S(1)} %get-tuple-element.51), channel_id=1, source_target_pairs={{8,0},{16,8},{24,16},{32,24},{40,32},{48,40},{56,48},{64,56},{72,6... | collective-permute-start | bytes 104456 | tf_op jit(solution)/shard_map/ppermute | solution.py:15
  631.8 2.0 copy-start
  631.8 2.3 copy-start.22
  634.1 1.2 copy-start.21
  635.3 1.2 copy-start.20
  636.6 1.2 copy-start.19
  637.8 1.2 copy-start.18
  640.2 1.2 copy-start.16
  641.5 1.2 copy-start.15
  642.7 1.2 copy-start.14
  643.9 1.2 copy-start.13
  645.1 1.2 copy-start.12
  646.4 1.2 copy-start.11
  648.8 1.2 copy-start.9
  650.0 1.2 copy-start.8
  651.3 1.2 copy-start.7
  652.5 1.2 copy-start.6
  653.7 1.2 copy-start.5
  656.2 1.2 copy-start.3
  (5 other events, 6.1 us)
Sparse Core Ops, SparseCore 0:
  366.4 265.3 all-reduce.1
where the time goes:
time: 681 us; the launch traced here: 670 us
  local copies, waits for them, and re-layouts  381 us (56%)
  waiting for transfers between devices  246 us (36%)
  between operations  13.7 us (2%)
  matrix products  10.3 us (2%)
  starting transfers between devices  9.44 us (1%)
  other arithmetic  7.83 us (1%)
    gather x384, local copies, waits for them, and re-layouts  348 us
    psum x1, waiting for transfers between devices, body(): whole = lax.psum(table, ('lon', 'lat'))  245 us
    unnamed x50, local copies, waits for them, and re-layouts  17.1 us
  transfers between devices with their start and end apart: 5, of which 3 were waited for; matrix products, arithmetic and copies ran while one was open for 55% of the time, Pallas kernels for 0%

commit v1 on v0

--- a/solution.py
+++ b/solution.py
@@ -33,7 +33,9 @@
     patches = jax.vmap(take, out_axes=3)(row_first, col_first).astype(jnp.float32)
     count = patches.shape[3]
     table = jnp.where((owner == here)[None, None, None, :], patches, 0.0)
-    whole = lax.psum(table, ("lon", "lat"))
+    whole = table
+    for nth in ("lon", "lat"):
+        whole = jax.lax.psum(whole, axis_name=nth)
     mean_sq = jnp.mean(whole * whole, axis=(0, 1, 2))
     queries = (whole * lax.rsqrt(mean_sq + 1e-05)).astype(jnp.bfloat16)
     extended = extended_2(embeddings, (("lat", 0), ("lon", 1)), 2)

time: 681 us -> 744 us (1.093)
  waiting for transfers between devices: 246 us -> 314 us
    psum x1 -> x2, waiting for transfers between devices: 245 us -> 309 us  [body(): whole = jax.lax.psum(whole, axis_name=nth)]
    unnamed x50 -> x52, local copies, waits for them, and re-layouts: 17.1 us -> 17.9 us
  transfers between devices with their start and end apart: 5 -> 6, of which waited for: 3 -> 6; matrix products, arithmetic and copies ran while one was open for 55% -> 2% of each run, Pallas kernels for 0% -> 0%
where the time goes in v1:
time: 744 us; the launch traced here: 733 us
  local copies, waits for them, and re-layouts  376 us (51%)
  waiting for transfers between devices  314 us (42%)
  between operations  13.7 us (2%)
  matrix products  10.3 us (1%)
  starting transfers between devices  9.01 us (1%)
  other arithmetic  7.82 us (1%)
    gather x384, local copies, waits for them, and re-layouts  344 us
    psum x2, waiting for transfers between devices, body(): whole = jax.lax.psum(whole, axis_name=nth)  309 us
    unnamed x52, local copies, waits for them, and re-layouts  17.9 us
  transfers between devices with their start and end apart: 6, of which 6 were waited for; matrix products, arithmetic and copies ran while one was open for 2% of the time, Pallas kernels for 0%

profile of v1, /device:TPU:2, one launch (start us, length us, event | category | flops | bytes accessed | tf_op | source)
XLA Modules:
  0.0 733.0 jit_solution(15044461541552999141)
XLA Ops:
  8.8 345.5 %while.1 = (s32[]{:T(128)}, bf16[64,64,128]{2,1,0:T(8,128)(2,1)}, s32[128,3]{0,1:T(4,128)S(1)}, bf16[128,5,5,128]{3,2,1,0:T(8,128)(2,1)S(1)}, s32[]{:T(128)}) while((s32[]{:T(128)}, bf16[64,64,128]{2,1,0:T(8,128)(2,1)}, s32[128,3]{0,1:T(4,128)S(1)}, bf16[128,5,5,128]{3,2,1,0:T(8,128)(2,1)S(1)}, s32[]{:T(128)}) %tuple.46), condition=%wide.while_cond, body=%wide.while_body.sunk | while | flops 2 | bytes 16765 | solution.py:31
  9.5 2.0 bitcast_dynamic-update-slice_fusion.2
  14.9 2.0 bitcast_dynamic-update-slice_fusion.2
  17.7 2.0 bitcast_dynamic-update-slice_fusion.2
  25.8 2.0 bitcast_dynamic-update-slice_fusion.2
  33.9 2.0 bitcast_dynamic-update-slice_fusion.2
  42.0 2.0 bitcast_dynamic-update-slice_fusion.2
  47.4 2.0 bitcast_dynamic-update-slice_fusion.2
  55.5 2.0 bitcast_dynamic-update-slice_fusion.2
  63.6 2.0 bitcast_dynamic-update-slice_fusion.2
  77.1 2.0 bitcast_dynamic-update-slice_fusion.2
  82.5 2.0 bitcast_dynamic-update-slice_fusion.2
  90.6 2.0 bitcast_dynamic-update-slice_fusion.2
  147.3 2.0 bitcast_dynamic-update-slice_fusion.2
  266.0 2.0 bitcast_dynamic-update-slice_fusion.2
  349.7 2.0 bitcast_dynamic-update-slice_fusion.2
  357.4 3.2 collective-permute-start
  363.9 2.2 collective-permute-done.1
  366.2 4.4 collective-permute-start.3
  373.6 211.7 %all-reduce.3.cloned.1.call-done = f32[5,5,128,128]{3,2,1,0:T(8,128)} async-done(((f32[5,5,128,128]{3,2,1,0:T(8,128)}), f32[5,5,128,128]{3,2,1,0:T(8,128)}) %all-reduce.3.cloned.1.call-update) | async-done | bytes 1638416 | tf_op jit(solution)/shard_map/psum | solution.py:38
  585.6 3.5 fusion.7
  589.0 7.7 %fusion.6 = (bf16[64,64,128]{2,1,0:T(8,128)(2,1)S(1)}, bf16[64,64,128]{2,1,0:T(8,128)(2,1)S(1)}, bf16[64,64,128]{2,1,0:T(8,128)(2,1)}, bf16[64,64,128]{2,1,0:T(8...) fusion(bf16[68,68,128]{2,1,0:T(8,128)(2,1)S(1)} %get-tuple-elem, ...), kind=kLoop, calls=%fused_computation.96 | loop fusion | bytes 39845888 | tf_op jit(solution)/shard_map/slice | solution.py:49
  596.7 97.0 %all-reduce.5.cloned.1.call-done = f32[5,5,128,128]{3,2,1,0:T(8,128)} async-done(((f32[5,5,128,128]{3,2,1,0:T(8,128)}), f32[5,5,128,128]{3,2,1,0:T(8,128)}) %all-reduce.5.cloned.1.call-update) | async-done | bytes 1638416 | tf_op jit(solution)/shard_map/psum | solution.py:38
  693.7 2.0 multiply_reduce_fusion.1
  (474 shorter events, 355.5 us)
Async XLA Ops:
  6.5 578.8 %all-reduce.3.cloned.1.call-start = ((), (), s32[]{:S(2)}) async-start(), calls=%async_computation | async-start | bytes 3276800 | tf_op jit(solution)/shard_map/psum | solution.py:38
  355.9 1.5 copy-start.24
  357.2 336.5 %all-reduce.5.cloned.1.call-start = ((), (), s32[]{:S(2)}) async-start(), calls=%async_computation.1 | async-start | bytes 3276800 | tf_op jit(solution)/shard_map/psum | solution.py:38
  357.4 6.4 collective-permute-start
  360.6 5.4 collective-permute-start.1
  366.1 6.0 collective-permute-start.2
  366.2 6.1 collective-permute-start.3
  693.7 2.0 copy-start
  693.7 2.3 copy-start.23
  696.0 1.2 copy-start.22
  697.2 1.2 copy-start.21
  698.4 1.2 copy-start.20
  699.7 1.2 copy-start.19
  700.9 1.2 copy-start.18
  702.1 1.2 copy-start.17
  704.6 1.2 copy-start.15
  705.8 1.2 copy-start.14
  707.0 1.2 copy-start.13
  708.2 1.2 copy-start.12
  709.5 1.2 copy-start.11
  711.9 1.2 copy-start.9
  713.1 1.2 copy-start.8
  714.4 1.2 copy-start.7
  715.6 1.2 copy-start.6
  (7 other events, 8.6 us)
Sparse Core Ops, SparseCore 0:
  357.4 227.8 all-reduce.2
  588.2 105.5 all-reduce.4
